TPU v7x, 256 devices: a whole 4x4x8 slice. The times are simulated.
256 devices in a mesh: seq: 32 (over x, y, core), tensor: 8 (over z).
Axes of the slice: x: 4, y: 4, z: 8, core: 2. Of those that a mesh axis runs over, the one named last changes fastest.
Arguments:
- tokens: bfloat16 [4, 4, 1600], replicated, may hold values from -6 to 6
- first_gain: float32 [1600], replicated, may hold values from 0.25 to 1.75
- first_shift: float32 [1600], replicated, may hold values from -3 to 3
- input_weight: bfloat16 [1600, 3, 2048], P(None, None, 'tensor'), may hold values from -0.15625 to 0.15625
- input_bias: float32 [3, 2048], P(None, 'tensor')
- output_weight: bfloat16 [2048, 1600], P('tensor'), may hold values from -0.125 to 0.125
- output_bias: float32 [1600], replicated, may hold values from -3 to 3
- second_gain: float32 [1600], replicated, may hold values from 0.25 to 1.75
- second_shift: float32 [1600], replicated, may hold values from -3 to 3
- expand_weight: bfloat16 [1600, 6400], P(None, 'tensor'), may hold values from -0.15625 to 0.15625
- expand_bias: float32 [6400], P('tensor'), may hold values from -3 to 3
- contract_weight: bfloat16 [6400, 1600], P('tensor'), may hold values from -0.078125 to 0.078125
- contract_bias: float32 [1600], replicated, may hold values from -3 to 3
- key_cache: bfloat16 [4, 16384, 2048], P(None, 'seq', 'tensor')
- value_cache: bfloat16 [4, 16384, 2048], P(None, 'seq', 'tensor'), may hold values from -6 to 6
- cache_fill: int32 [4, 32], replicated, may hold values from 0 to 508, as said below
- owner_shard: int32 [4, 4], replicated, may hold values from 0 to 31, as said below
Outputs:
- hidden_out: bfloat16 [4, 4, 1600], replicated
- new_keys: bfloat16 [4, 16384, 2048], P(None, 'seq', 'tensor')
- new_values: bfloat16 [4, 16384, 2048], P(None, 'seq', 'tensor')
Inputs may be any that keep to these rules, and one draw needn't show every extreme that they name: `cache_fill`: 1 request hold 506 to 508 entries on every shard; every other request holds 1 to 508 entries on one shard and none on the others. `owner_shard`: a request with entries on one shard only appends all its new tokens to that shard.
All inputs are finite; a program needn't handle non-finite values.
Results may differ from a plain program's by a relative error of at most 0.0046.
Values sent between devices are 32-bit elements; how exact they have to be, the bound alone decides.
A program may use at most 64 MiB of HBM per device.

v0:
```python
import math
import jax
import jax.numpy as jnp
from jax import lax
from jax.sharding import PartitionSpec as P

HEAD_DIM = 64


def layer_norm(values, gain, shift):
    center = values - jnp.mean(values, axis=-1, keepdims=True)
    spread = jnp.mean(center * center, axis=-1, keepdims=True)
    return center * lax.rsqrt(spread + 1e-05) * gain + shift


def widen_heads(per_head):
    return jnp.repeat(per_head, HEAD_DIM, axis=-1)


def attend(queries, key_rows, value_rows, live_count):
    rounds, requests, row_width = queries.shape
    head_count = row_width // HEAD_DIM
    slot_count = key_rows.shape[1]
    query_heads = queries.reshape(rounds, requests, head_count, HEAD_DIM)
    key_heads = key_rows.reshape(requests, slot_count, head_count, HEAD_DIM)
    value_heads = value_rows.reshape(requests, slot_count, head_count, HEAD_DIM)
    scores = jnp.einsum(
        "tbhd,bshd->tbhs", query_heads, key_heads, preferred_element_type=jnp.float32
    ) * (1.0 / math.sqrt(HEAD_DIM))
    usable = (lax.iota(jnp.int32, slot_count)[None, None, :] < live_count[:, :, None])[
        :, :, None, :
    ]
    peaks = jnp.max(jnp.where(usable, scores, -1e30), axis=-1)
    weights = jnp.where(usable, jnp.exp(scores - peaks[..., None]), 0.0)
    totals = jnp.sum(weights, axis=-1)
    blended = jnp.einsum(
        "tbhs,bshd->tbhd",
        weights.astype(jnp.bfloat16),
        value_heads,
        preferred_element_type=jnp.float32,
    )
    return (peaks, totals, blended.reshape(rounds, requests, row_width))


def merge_heads(parts):
    peaks, totals, blended = parts
    highest = lax.pmax(peaks, "seq")
    factor = jnp.exp(peaks - highest)
    totals, blended = lax.psum((totals * factor, blended * widen_heads(factor)), "seq")
    return (blended / widen_heads(totals)).astype(jnp.bfloat16)


def project_in(rows, first_gain, first_shift, input_weight, input_bias):
    normed = layer_norm(rows.astype(jnp.float32), first_gain, first_shift).astype(jnp.bfloat16)
    packed = (
        jnp.einsum("rd,dch->rch", normed, input_weight, preferred_element_type=jnp.float32)
        + input_bias
    )
    return packed.astype(jnp.bfloat16)


def finish(
    rows,
    attended,
    output_weight,
    output_bias,
    second_gain,
    second_shift,
    expand_weight,
    expand_bias,
    contract_weight,
    contract_bias,
):
    heads_sum = lax.psum(
        jnp.dot(attended, output_weight, preferred_element_type=jnp.float32), "tensor"
    )
    middle = rows.astype(jnp.float32) + heads_sum + output_bias
    second = layer_norm(middle, second_gain, second_shift).astype(jnp.bfloat16)
    hidden = jax.nn.gelu(
        jnp.dot(second, expand_weight, preferred_element_type=jnp.float32) + expand_bias,
        approximate=True,
    ).astype(jnp.bfloat16)
    units_sum = lax.psum(
        jnp.dot(hidden, contract_weight, preferred_element_type=jnp.float32), "tensor"
    )
    return (units_sum + contract_bias + middle).astype(jnp.bfloat16)


def write_cache(cache, fresh_rows, slot_index, owned):
    slot_count = cache.shape[1]
    places = (lax.iota(jnp.int32, slot_count)[None, :] == slot_index[:, None]) & (
        owned[:, None] > 0
    )
    return jnp.where(places[:, :, None], fresh_rows[:, None, :], cache)


def per_device(
    tokens,
    first_gain,
    first_shift,
    input_weight,
    input_bias,
    output_weight,
    output_bias,
    second_gain,
    second_shift,
    expand_weight,
    expand_bias,
    contract_weight,
    contract_bias,
    key_cache,
    value_cache,
    cache_fill,
    owner_shard,
):
    shard = lax.axis_index("seq")
    shard_count = cache_fill.shape[1]
    picked = lax.iota(jnp.int32, shard_count)[None, :] == shard
    own_fill = jnp.sum(jnp.where(picked, cache_fill, 0), axis=1)
    owned = (owner_shard == shard).astype(jnp.int32)
    through = jnp.cumsum(owned, axis=0)
    slot_index = own_fill[None, :] + through - owned
    live_count = own_fill[None, :] + through
    step_total, requests, model_width = tokens.shape
    outputs = []
    for step_index in range(step_total):
        packed = project_in(tokens[step_index], first_gain, first_shift, input_weight, input_bias)
        key_cache = write_cache(key_cache, packed[:, 1], slot_index[step_index], owned[step_index])
        value_cache = write_cache(
            value_cache, packed[:, 2], slot_index[step_index], owned[step_index]
        )
        parts = attend(
            packed[None, :, 0], key_cache, value_cache, live_count[step_index : step_index + 1]
        )
        attended = merge_heads(parts)[0]
        outputs.append(
            finish(
                tokens[step_index],
                attended,
                output_weight,
                output_bias,
                second_gain,
                second_shift,
                expand_weight,
                expand_bias,
                contract_weight,
                contract_bias,
            )
        )
    hidden_out = jnp.stack(outputs)
    return (hidden_out, key_cache, value_cache)


def solution(mesh):
    return jax.shard_map(
        per_device,
        mesh=mesh,
        in_specs=(
            P(),
            P(),
            P(),
            P(None, None, "tensor"),
            P(None, "tensor"),
            P("tensor", None),
            P(),
            P(),
            P(),
            P(None, "tensor"),
            P("tensor"),
            P("tensor", None),
            P(),
            P(None, "seq", "tensor"),
            P(None, "seq", "tensor"),
            P(),
            P(),
        ),
        out_specs=(P(), P(None, "seq", "tensor"), P(None, "seq", "tensor")),
        check_vma=False,
    )
```

profile of v0, /device:TPU:2, one launch (start us, length us, event | category | flops | bytes accessed | tf_op | source)
XLA Modules:
  0.0 433.3 jit_solution(10217517019822369008)
XLA Ops:
  7.3 0.8 compare_convert_fusion
  8.2 1.1 convert_reduce_fusion
  9.3 1.0 fusion.28
  10.3 2.2 fusion.3
  12.6 0.5 fusion.2
  13.1 0.5 fusion.1
  13.5 2.3 copy.25
  15.8 2.2 fusion
  18.0 2.3 copy.24
  20.4 0.1 select_reduce_fusion.4
  20.9 4.8 %broadcast_select_fusion = (bf16[4,512,256]{1,2,0:T(8,128)(2,1)S(1)}, bf16[4,512,256]{1,2,0:T(8,128)(2,1)}, bf16[4,512,256]{1,2,0:T(8,128)(2,1)}, bf16[4,512,256...) fusion(pred[4,512]{1,0:T(4,128)(4,1)S(1)} %fusion.151, ...), kind=kLoop, calls=%fused_computation.12 | loop fusion | flops 4194304 | bytes 10510336 | tf_op jit(solution)/shard_map/jit(_where)/select_n | solution.py:94
  25.7 1.0 copy-done.3
  26.7 0.2 fusion.224
  27.1 0.7 fusion.147
  28.2 1.5 fusion.223
  29.9 1.3 fusion.146
  31.2 1.5 fusion.222
  32.7 1.3 fusion.145
  34.0 1.5 fusion.221
  35.6 1.3 fusion.144
  36.9 1.0 fusion.12
  37.8 57.0 %all-reduce.1 = (f32[1,4,4]{2,1,0:T(4,128)}, f32[1,4,4]{2,1,0:T(4,128)}, f32[1,4,4]{2,1,0:T(4,128)}, f32[1,4,4]{2,1,0:T(4,128)}) all-reduce(f32[1,4,4]{2,1,0:T(4,128)S(1)} %bitcast.321, f32[1,4,4]{2,1,0:T(4,128)S(1)} %bitcast.323, f32[1,4,4]{2,1,0:T(4,128)S(1)} %bitcast.322, ...), channel_id=1, replica_groups=mesh['seq'=32,'tensor'=8] {'seq'}, use_global_device_ids=true, to_apply=%region_38.39 | all-reduce | flops 64 | bytes 512 | tf_op jit(solution)/shard_map/pmax | solution.py:47
  94.8 1.3 fusion.178
  96.1 1.4 broadcast_multiply_fusion
  97.4 1.4 mul.328
  98.8 1.6 fusion.14
  100.4 1.3 fusion.181
  101.8 0.7 mul.312
  102.4 1.6 fusion.16
  104.0 1.3 fusion.184
  105.4 0.7 broadcast_multiply_fusion.2
  106.0 1.4 mul.296
  107.4 1.6 fusion.18
  109.0 1.3 fusion.187
  110.3 0.7 broadcast_multiply_fusion.3
  111.0 1.4 mul.279
  112.4 118.0 %all-reduce = (f32[1,4,256]{2,1,0:T(4,128)}, f32[4,4]{1,0:T(4,128)}, f32[1,4,256]{2,1,0:T(4,128)}, f32[4,4]{1,0:T(4,128)}, f32[1,4,256]{2,1,0:T(4,128)}, /*index...) all-reduce(f32[1,4,256]{2,1,0:T(4,128)} %mul.328, ...), channel_id=1, replica_groups=mesh['seq'=32,'tensor'=8] {'seq'}, use_global_device_ids=true, to_apply=%region_39.40 | all-reduce | flops 4160 | bytes 33280 | tf_op jit(solution)/shard_map/psum | solution.py:49
  230.3 1.4 broadcast_in_dim.307
  231.7 1.4 broadcast_in_dim.308
  233.1 1.3 broadcast_in_dim.298
  234.4 1.4 broadcast_in_dim.299
  235.8 1.3 broadcast_in_dim.289
  237.1 1.4 broadcast_in_dim.290
  238.5 1.3 broadcast_in_dim.280
  239.8 1.4 broadcast_in_dim.281
  241.2 1.6 fusion.176
  242.8 1.6 fusion.179
  244.5 1.6 fusion.182
  246.1 1.6 fusion.185
  247.8 88.4 %all-reduce.9.cloned.1.call-done = (f32[4,1600]{1,0:T(4,128)}, f32[4,1600]{1,0:T(4,128)}, f32[4,1600]{1,0:T(4,128)}, f32[4,1600]{1,0:T(4,128)}) async-done(((f32[4,1600]{1,0:T(4,128)}, f32[4,1600]{1,0:T(4,128)}, f32[4,1600]{1,0:T(4,128)}, f32[4,1600]{1,0:T(4,128)}), (f32[4,1600]{1,0:T(4,128)}, f32[4,1600]{1,0:T(4,128)}, f32[4,1600]{1,0:T(4,128)}, f32[4,1600]{1,0:T(4,128)})) %all-reduce.9.cloned.1.call-update) | async-done | bytes 102416 | tf_op jit(solution)/shard_map/psum | solution.py:74
  336.2 1.0 fusion.208
  337.2 0.2 multiply_reduce_fusion
  337.4 0.2 multiply_reduce_fusion.1
  337.7 3.9 fusion.83
  341.6 3.9 fusion.74
  345.5 0.2 multiply_reduce_fusion.2
  345.7 3.9 fusion.65
  349.6 0.2 multiply_reduce_fusion.3
  349.8 3.9 fusion.56
  353.8 2.3 copy.26
  356.0 2.3 copy.27
  358.3 66.6 %all-reduce.7.cloned.1.call-done = (f32[4,1600]{1,0:T(4,128)}, f32[4,1600]{1,0:T(4,128)}, f32[4,1600]{1,0:T(4,128)}, f32[4,1600]{1,0:T(4,128)}) async-done(((f32[4,1600]{1,0:T(4,128)}, f32[4,1600]{1,0:T(4,128)}, f32[4,1600]{1,0:T(4,128)}, f32[4,1600]{1,0:T(4,128)}), (f32[4,1600]{1,0:T(4,128)}, f32[4,1600]{1,0:T(4,128)}, f32[4,1600]{1,0:T(4,128)}, f32[4,1600]{1,0:T(4,128)})) %all-reduce.7.cloned.1.call-update) | async-done | bytes 102416 | tf_op jit(solution)/shard_map/psum | solution.py:83
  424.9 0.8 fusion.84
  425.7 0.7 pad_maximum_fusion
  (79 shorter events, 1.8 us)
Async XLA Ops:
  7.2 330.4 %copy-start = (bf16[800,1600]{1,0:T(8,128)(2,1)S(1)}, bf16[800,1600]{1,0:T(8,128)(2,1)}, u32[]{:S(2)}) copy-start(bf16[800,1600]{1,0:T(8,128)(2,1)} %param.28) | copy-start | bytes 7680004
  7.2 5.3 %copy-start.5 = (bf16[4,4,1600]{2,1,0:T(4,128)(2,1)S(1)}, bf16[4,4,1600]{2,1,0:T(4,128)(2,1)}, u32[]{:S(2)}) copy-start(bf16[4,4,1600]{2,1,0:T(4,128)(2,1)} %param.17) | copy-start | bytes 153604
  7.2 5.3 %copy-start.6 = (f32[1600]{0:T(1024)S(1)}, f32[1600]{0:T(1024)}, u32[]{:S(2)}) copy-start(f32[1600]{0:T(1024)} %param.19) | copy-start | bytes 19204
  7.2 5.3 %copy-start.7 = (f32[1600]{0:T(1024)S(1)}, f32[1600]{0:T(1024)}, u32[]{:S(2)}) copy-start(f32[1600]{0:T(1024)} %param.18) | copy-start | bytes 19204
  7.2 5.3 %copy-start.10 = (f32[3,256]{1,0:T(4,128)S(1)}, f32[3,256]{1,0:T(4,128)}, u32[]{:S(2)}) copy-start(f32[3,256]{1,0:T(4,128)} %param.21) | copy-start | bytes 9220
  7.2 329.0 %all-reduce.9.cloned.1.call-start = ((), (), s32[]{:S(2)}) async-start(), calls=%async_computation.1 | async-start | bytes 212992 | tf_op jit(solution)/shard_map/psum | solution.py:74
  8.2 4.4 %copy-start.1 = (bf16[1600,3,256]{2,0,1:T(8,128)(2,1)S(1)}, bf16[1600,3,256]{2,0,1:T(8,128)(2,1)}, u32[]{:S(2)}) copy-start(bf16[1600,3,256]{2,0,1:T(8,128)(2,1)} %param.20) | copy-start | bytes 7372804
  15.8 4.6 %copy-start.17 = (s32[4,32]{1,0:T(4,128)S(1)}, s32[4,32]{1,0:T(4,128)}, u32[]{:S(2)}) copy-start(s32[4,32]{1,0:T(4,128)} %param.32) | copy-start | bytes 1540
  15.8 4.7 %copy-start.16 = (s32[4,4]{1,0:T(4,128)S(1)}, s32[4,4]{1,0:T(4,128)}, u32[]{:S(2)}) copy-start(s32[4,4]{1,0:T(4,128)} %param.33) | copy-start | bytes 196
  25.7 1.0 copy-start.3
  28.2 8.7 %copy-start.4 = (bf16[4,512,256]{1,2,0:T(8,128)(2,1)S(1)}, bf16[4,512,256]{1,2,0:T(8,128)(2,1)}, u32[]{:S(2)}) copy-start(bf16[4,512,256]{1,2,0:T(8,128)(2,1)} %get-tuple-element.73) | copy-start | bytes 3145732
  28.2 8.7 %copy-start.14 = (bf16[4,4,512,1]{2,1,0,3:T(4,128)(2,1)S(1)}, bf16[4,4,512,1]{2,1,0,3:T(4,128)(2,1)}, u32[]{:S(2)}) copy-start(bf16[4,4,512,1]{2,1,0,3:T(4,128)(2,1)} %get-tuple-element.68) | copy-start | bytes 49156
  32.7 69.7 %copy-start.13 = (f32[4,4]{1,0:T(4,128)}, f32[4,4]{1,0:T(4,128)S(1)}, u32[]{:S(2)}) copy-start(f32[4,4]{1,0:T(4,128)S(1)} %select_reduce_fusion.2) | copy-start | bytes 196
  35.5 205.7 %copy-start.2 = (bf16[256,1600]{0,1:T(8,128)(2,1)S(1)}, bf16[256,1600]{0,1:T(8,128)(2,1)}, u32[]{:S(2)}) copy-start(bf16[256,1600]{0,1:T(8,128)(2,1)} %param.22) | copy-start | bytes 2457604
  35.6 66.9 %copy-start.12 = (f32[4,4]{1,0:T(4,128)}, f32[4,4]{1,0:T(4,128)S(1)}, u32[]{:S(2)}) copy-start(f32[4,4]{1,0:T(4,128)S(1)} %select_reduce_fusion.3) | copy-start | bytes 196
  104.0 233.6 %copy-start.8 = (f32[1600]{0:T(1024)S(1)}, f32[1600]{0:T(1024)}, u32[]{:S(2)}) copy-start(f32[1600]{0:T(1024)} %param.25) | copy-start | bytes 19204
  104.0 233.6 %copy-start.9 = (f32[1600]{0:T(1024)S(1)}, f32[1600]{0:T(1024)}, u32[]{:S(2)}) copy-start(f32[1600]{0:T(1024)} %param.24) | copy-start | bytes 19204
  104.0 233.6 %copy-start.11 = (f32[800]{0:T(1024)S(1)}, f32[800]{0:T(1024)}, u32[]{:S(2)}) copy-start(f32[800]{0:T(1024)} %param.27) | copy-start | bytes 9604
  247.7 177.2 %all-reduce.7.cloned.1.call-start = ((), (), s32[]{:S(2)}) async-start(), calls=%async_computation | async-start | bytes 212992 | tf_op jit(solution)/shard_map/psum | solution.py:83
  353.8 71.2 %copy-start.15 = (f32[1600]{0:T(1024)S(1)}, f32[1600]{0:T(1024)}, u32[]{:S(2)}) copy-start(f32[1600]{0:T(1024)} %param.29) | copy-start | bytes 19204
Sparse Core Ops, SparseCore 0:
  247.9 88.2 all-reduce.8
  353.9 70.9 all-reduce.6
where the time goes:
time: 435 us; the launch traced here: 433 us
  blocking collectives  175 us (40%)
  waiting for transfers between devices  155 us (36%)
  matrix products  38 us (9%)
  local copies, waits for them, and re-layouts  26.2 us (6%)
  other arithmetic  24.7 us (6%)
  between operations  14.3 us (3%)
    psum x1, blocking collectives, merge_heads(): lax.psum((totals * factor, blended * widen_heads(factor)), 'seq')  118 us
    psum x1, waiting for transfers between devices, finish(): lax.psum(jnp.dot(attended, output_weight, preferred_element_type=jnp.floa...  88.4 us
    psum x1, waiting for transfers between devices, finish(): lax.psum(jnp.dot(hidden, contract_weight, preferred_element_type=jnp.floa...  66.6 us
    pmax x1, blocking collectives, merge_heads(): highest = lax.pmax(peaks, 'seq')  57 us
    dot_general x4, matrix products, finish(): jnp.dot(hidden, contract_weight, preferred_element_type=jnp.float32)  15.7 us
    broadcast_in_dim x8, local copies, waits for them, and re-layouts, widen_heads(): return jnp.repeat(per_head, HEAD_DIM, axis=-1)  10.9 us
    unnamed x40, local copies, waits for them, and re-layouts  10.2 us
  transfers between devices with their start and end apart: 2, of which 2 were waited for; matrix products, arithmetic and copies ran while one was open for 1% of the time, Pallas kernels for 0%

commit v1 on v0

--- a/solution.py
+++ b/solution.py
@@ -5,6 +5,7 @@
 from jax.sharding import PartitionSpec as P
 
 HEAD_DIM = 64
+remake_the_record = lambda view, ax_name: lax.all_gather(view, axis_name=ax_name).sum(axis=0)
 
 
 def layer_norm(values, gain, shift):
@@ -71,7 +72,7 @@
     contract_weight,
     contract_bias,
 ):
-    heads_sum = lax.psum(
+    heads_sum = remake_the_record(
         jnp.dot(attended, output_weight, preferred_element_type=jnp.float32), "tensor"
     )
     middle = rows.astype(jnp.float32) + heads_sum + output_bias

time: 435 us -> 462 us (1.062)
  blocking collectives: 175 us -> 284 us
  waiting for transfers between devices: 155 us -> 80.3 us
  local copies, waits for them, and re-layouts: 26.2 us -> 20.7 us
    all_gather x0 -> x4, blocking collectives: none -> 109 us  [lax.all_gather(view, axis_name=ax_name).sum(axis=0)]
    psum x1 -> x0, waiting for transfers between devices: 88.4 us -> none  [finish(): lax.psum(jnp.dot(attended, output_weight, preferred_element_type=jnp.floa...]
    psum x1, waiting for transfers between devices: 66.6 us -> 80.3 us  [finish(): lax.psum(jnp.dot(hidden, contract_weight, preferred_element_type=jnp.floa...]
    reduce_sum x0 -> x4, other arithmetic: none -> 4.79 us  [lax.all_gather(view, axis_name=ax_name).sum(axis=0)]
    unnamed x40 -> x30, local copies, waits for them, and re-layouts: 10.2 us -> 9.14 us
  transfers between devices with their start and end apart: 2 -> 1, of which waited for: 2 -> 1; matrix products, arithmetic and copies ran while one was open for 1% -> 1% of each run, Pallas kernels for 0% -> 0%
where the time goes in v1:
time: 462 us; the launch traced here: 460 us
  blocking collectives  284 us (61%)
  waiting for transfers between devices  80.3 us (17%)
  matrix products  35 us (8%)
  other arithmetic  26.2 us (6%)
  local copies, waits for them, and re-layouts  20.7 us (4%)
  between operations  14.3 us (3%)
    psum x1, blocking collectives, merge_heads(): lax.psum((totals * factor, blended * widen_heads(factor)), 'seq')  118 us
    all_gather x4, blocking collectives, lax.all_gather(view, axis_name=ax_name).sum(axis=0)  109 us
    psum x1, waiting for transfers between devices, finish(): lax.psum(jnp.dot(hidden, contract_weight, preferred_element_type=jnp.floa...  80.3 us
    pmax x1, blocking collectives, merge_heads(): highest = lax.pmax(peaks, 'seq')  57 us
    dot_general x4, matrix products, finish(): jnp.dot(hidden, contract_weight, preferred_element_type=jnp.float32)  15.7 us
  transfers between devices with their start and end apart: 1, of which 1 were waited for; matrix products, arithmetic and copies ran while one was open for 1% of the time, Pallas kernels for 0%

profile of v1, /device:TPU:2, one launch (start us, length us, event | category | flops | bytes accessed | tf_op | source)
XLA Modules:
  0.0 460.4 jit_solution(12109323459616348327)
XLA Ops:
  7.3 1.1 convert_reduce_fusion
  8.4 1.1 fusion.28
  9.5 2.2 fusion
  11.7 1.2 fusion.1
  13.0 0.5 fusion.2
  13.5 0.5 fusion.3
  14.1 2.3 copy.28
  16.4 2.3 copy.29
  18.7 0.1 select_reduce_fusion.4
  19.3 4.8 %broadcast_select_fusion = (bf16[4,512,256]{1,2,0:T(8,128)(2,1)}, bf16[4,512,256]{1,2,0:T(8,128)(2,1)}, bf16[4,512,256]{1,2,0:T(8,128)(2,1)}, bf16[4,512,256]{1,...) fusion(pred[4,512]{1,0:T(4,128)(4,1)S(1)} %fusion.151, ...), kind=kLoop, calls=%fused_computation.16 | loop fusion | flops 4194304 | bytes 10510336 | tf_op jit(solution)/shard_map/jit(_where)/select_n | solution.py:95
  24.0 0.2 fusion.217
  24.3 0.1 select_reduce_fusion.3
  24.4 0.7 fusion.144
  25.5 1.5 fusion.218
  27.1 1.3 fusion.145
  28.4 1.5 fusion.219
  29.9 1.3 fusion.146
  31.2 1.5 fusion.220
  32.8 1.3 fusion.147
  34.1 57.0 %all-reduce.1 = (f32[1,4,4]{2,1,0:T(4,128)}, f32[1,4,4]{2,1,0:T(4,128)}, f32[1,4,4]{2,1,0:T(4,128)}, f32[1,4,4]{2,1,0:T(4,128)}) all-reduce(f32[1,4,4]{2,1,0:T(4,128)S(1)} %bitcast.328, f32[1,4,4]{2,1,0:T(4,128)S(1)} %bitcast.330, f32[1,4,4]{2,1,0:T(4,128)S(1)} %bitcast.331, ...), channel_id=1, replica_groups=mesh['seq'=32,'tensor'=8] {'seq'}, use_global_device_ids=true, to_apply=%region_38.39 | all-reduce | flops 64 | bytes 512 | tf_op jit(solution)/shard_map/pmax | solution.py:48
  91.1 1.2 fusion.183
  92.3 1.6 fusion.18
  93.9 0.7 broadcast_multiply_fusion.3
  94.6 1.4 mul.279
  95.9 1.3 fusion.181
  97.2 1.6 fusion.16
  98.9 0.7 mul.296
  99.6 0.7 fusion.179
  100.3 1.6 fusion.14
  102.0 1.3 fusion.177
  103.3 1.6 fusion.12
  105.1 118.0 %all-reduce = (f32[1,4,256]{2,1,0:T(4,128)}, f32[4,4]{1,0:T(4,128)}, f32[1,4,256]{2,1,0:T(4,128)}, f32[4,4]{1,0:T(4,128)}, f32[1,4,256]{2,1,0:T(4,128)}, /*index...) all-reduce(f32[1,4,256]{2,1,0:T(4,128)S(1)} %mul.328, ...), channel_id=1, replica_groups=mesh['seq'=32,'tensor'=8] {'seq'}, use_global_device_ids=true, to_apply=%region_39.40 | all-reduce | flops 4160 | bytes 33280 | tf_op jit(solution)/shard_map/psum | solution.py:50
  223.1 0.7 broadcast_in_dim.307
  223.9 1.0 convolution_bitcast_fusion
  224.9 30.5 %all-gather.7 = f32[8,4,1600]{2,1,0:T(4,128)} all-gather(f32[1,4,1600]{2,1,0:T(4,128)S(1)} %convolution_bitcast_fusion), channel_id=5, replica_groups=mesh['seq'=32,'tensor'=8] {'tensor'}, dimensions={0}, use_global_device_ids=true | all-gather | bytes 230400 | tf_op jit(solution)/shard_map/all_gather | solution.py:8
  255.5 1.3 broadcast_in_dim.298
  256.8 1.4 broadcast_in_dim.299
  258.2 1.0 convolution_bitcast_fusion.1
  259.2 26.7 %all-gather.6 = f32[8,4,1600]{2,1,0:T(4,128)} all-gather(f32[1,4,1600]{2,1,0:T(4,128)S(1)} %convolution_bitcast_fusion.1), channel_id=4, replica_groups=mesh['seq'=32,'tensor'=8] {'tensor'}, dimensions={0}, use_global_device_ids=true | all-gather | bytes 230400 | tf_op jit(solution)/shard_map/all_gather | solution.py:8
  285.9 1.6 reduce_sum.259
  287.5 1.6 reduce_sum.252
  289.1 1.3 broadcast_in_dim.289
  290.4 1.4 broadcast_in_dim.290
  291.8 1.0 convolution_bitcast_fusion.2
  292.8 26.8 %all-gather.5 = f32[8,4,1600]{2,1,0:T(4,128)} all-gather(f32[1,4,1600]{2,1,0:T(4,128)S(1)} %convolution_bitcast_fusion.2), channel_id=3, replica_groups=mesh['seq'=32,'tensor'=8] {'tensor'}, dimensions={0}, use_global_device_ids=true | all-gather | bytes 230400 | tf_op jit(solution)/shard_map/all_gather | solution.py:8
  319.6 1.6 reduce_sum.245
  321.1 1.3 broadcast_in_dim.280
  322.5 1.4 broadcast_in_dim.281
  323.8 1.0 convolution_bitcast_fusion.3
  324.8 24.7 %all-gather.4 = f32[8,4,1600]{2,1,0:T(4,128)S(1)} all-gather(f32[1,4,1600]{2,1,0:T(4,128)S(1)} %convolution_bitcast_fusion.3), channel_id=2, replica_groups=mesh['seq'=32,'tensor'=8] {'tensor'}, dimensions={0}, use_global_device_ids=true | all-gather | bytes 230400 | tf_op jit(solution)/shard_map/all_gather | solution.py:8
  349.6 1.0 fusion.204
  350.6 0.2 multiply_reduce_fusion.3
  350.8 0.2 multiply_reduce_fusion.2
  351.1 3.9 fusion.56
  355.0 3.9 fusion.65
  358.9 0.2 multiply_reduce_fusion.1
  359.1 3.9 fusion.74
  363.0 0.2 multiply_reduce_fusion
  363.2 3.9 fusion.83
  367.2 2.3 copy.30
  369.4 2.3 copy.31
  371.7 80.3 %all-reduce.5.cloned.1.call-done = (f32[4,1600]{1,0:T(4,128)}, f32[4,1600]{1,0:T(4,128)}, f32[4,1600]{1,0:T(4,128)}, f32[4,1600]{1,0:T(4,128)}) async-done(((f32[4,1600]{1,0:T(4,128)}, f32[4,1600]{1,0:T(4,128)}, f32[4,1600]{1,0:T(4,128)}, f32[4,1600]{1,0:T(4,128)}), (f32[4,1600]{1,0:T(4,128)}, f32[4,1600]{1,0:T(4,128)}, f32[4,1600]{1,0:T(4,128)}, f32[4,1600]{1,0:T(4,128)})) %all-reduce.5.cloned.1.call-update) | async-done | bytes 102416 | tf_op jit(solution)/shard_map/psum | solution.py:84
  452.0 0.8 fusion.84
  452.9 0.7 pad_maximum_fusion
  (74 shorter events, 2.1 us)
Async XLA Ops:
  7.2 343.8 %copy-start = (bf16[800,1600]{1,0:T(8,128)(2,1)S(1)}, bf16[800,1600]{1,0:T(8,128)(2,1)}, u32[]{:S(2)}) copy-start(bf16[800,1600]{1,0:T(8,128)(2,1)} %param.28) | copy-start | bytes 7680004
  7.2 5.8 %copy-start.3 = (bf16[4,4,1600]{2,1,0:T(4,128)(2,1)S(1)}, bf16[4,4,1600]{2,1,0:T(4,128)(2,1)}, u32[]{:S(2)}) copy-start(bf16[4,4,1600]{2,1,0:T(4,128)(2,1)} %param.17) | copy-start | bytes 153604
  7.2 5.8 %copy-start.5 = (f32[1600]{0:T(1024)S(1)}, f32[1600]{0:T(1024)}, u32[]{:S(2)}) copy-start(f32[1600]{0:T(1024)} %param.18) | copy-start | bytes 19204
  7.2 5.8 %copy-start.4 = (f32[1600]{0:T(1024)S(1)}, f32[1600]{0:T(1024)}, u32[]{:S(2)}) copy-start(f32[1600]{0:T(1024)} %param.19) | copy-start | bytes 19204
  7.2 5.8 %copy-start.8 = (f32[3,256]{1,0:T(4,128)S(1)}, f32[3,256]{1,0:T(4,128)}, u32[]{:S(2)}) copy-start(f32[3,256]{1,0:T(4,128)} %param.21) | copy-start | bytes 9220
  7.2 444.8 %all-reduce.5.cloned.1.call-start = ((), (), s32[]{:S(2)}) async-start(), calls=%async_computation | async-start | bytes 212992 | tf_op jit(solution)/shard_map/psum | solution.py:84
  7.3 4.5 copy-start.1
  13.0 1.1 copy-start.11
  14.0 4.7 %copy-start.12 = (s32[4,32]{1,0:T(4,128)S(1)}, s32[4,32]{1,0:T(4,128)}, u32[]{:S(2)}) copy-start(s32[4,32]{1,0:T(4,128)} %param.32) | copy-start | bytes 1540
  32.7 191.2 %copy-start.2 = (bf16[256,1600]{0,1:T(8,128)(2,1)S(1)}, bf16[256,1600]{0,1:T(8,128)(2,1)}, u32[]{:S(2)}) copy-start(bf16[256,1600]{0,1:T(8,128)(2,1)} %param.22) | copy-start | bytes 2457604
  224.9 126.1 %copy-start.6 = (f32[1600]{0:T(1024)S(1)}, f32[1600]{0:T(1024)}, u32[]{:S(2)}) copy-start(f32[1600]{0:T(1024)} %param.25) | copy-start | bytes 19204
  224.9 126.1 %copy-start.7 = (f32[1600]{0:T(1024)S(1)}, f32[1600]{0:T(1024)}, u32[]{:S(2)}) copy-start(f32[1600]{0:T(1024)} %param.24) | copy-start | bytes 19204
  224.9 126.1 %copy-start.9 = (f32[800]{0:T(1024)S(1)}, f32[800]{0:T(1024)}, u32[]{:S(2)}) copy-start(f32[800]{0:T(1024)} %param.27) | copy-start | bytes 9604
  367.1 84.9 %copy-start.10 = (f32[1600]{0:T(1024)S(1)}, f32[1600]{0:T(1024)}, u32[]{:S(2)}) copy-start(f32[1600]{0:T(1024)} %param.29) | copy-start | bytes 19204
Sparse Core Ops, SparseCore 0:
  367.3 84.6 all-reduce.4
